TPU v7x, 32 devices: a whole 2x2x4 slice. The times are simulated.
32 devices in a mesh: seq: 16 (over z, x, core), ex: 2 (over y).
Axes of the slice: x: 2, y: 2, z: 4, core: 2. Of those that a mesh axis runs over, the one named last changes fastest.
Arguments:
- acts: bfloat16 [4, 2048, 4096], P('ex', 'seq'), may hold values from -6 to 6
- out_grads: bfloat16 [4, 2048, 5120], P('ex', 'seq'), may hold values from -6 to 6
- lengths: int32 [4], P('ex'), may hold values from 512 to 2048, as said below
- in_tiles: bfloat16 [32, 128, 128], replicated, may hold values from -0.09375 to 0.09375
- in_blocks: int32 [32], replicated, may hold values from 0 to 31, each once
- in_signs: int32 [32, 128], replicated, may hold values 0 or 1
- out_tiles: bfloat16 [40, 128, 64], replicated, may hold values from -0.09375 to 0.09375
- out_blocks: int32 [40], replicated, may hold values from 0 to 39, as said below
- out_signs: int32 [40, 128], replicated, may hold values 0 or 1
- query_grads: bfloat16 [2048, 8192], P('seq', 'ex'), may hold values from -6 to 6
Outputs:
- scores: float32 [4, 2048], P('ex', 'seq')
Inputs may be any that keep to these rules, and one draw needn't show every extreme that they name: `lengths`: every training sequence has at least 512 live positions and some sequence has all 2048. `in_blocks`: a permutation of the 32 input feature blocks. `out_blocks`: the first 32 entries are a permutation of 0 to 31, the last 8 a permutation of 32 to 39.
All inputs are finite; a program needn't handle non-finite values.
Results may differ from a plain program's by a relative error of at most 0.005.
Values may be sent and summed in bfloat16 or wider, within the bound.
A program may use at most 64 MiB of HBM per device.

v0:
```python
import jax
import jax.numpy as jnp
from jax import lax
from jax.sharding import PartitionSpec as P


def place(sketch_tiles, block_ids, sign_bits):
    tile_count = sketch_tiles.shape[0]
    chosen = (block_ids[:, None] == jnp.arange(tile_count, dtype=jnp.int32)[None, :]).astype(
        jnp.float32
    )
    signed = sketch_tiles.astype(jnp.float32) * (2 * sign_bits - 1).astype(jnp.float32)[:, :, None]
    placed = jnp.einsum("bc,bik->cik", chosen, signed, precision=lax.Precision.HIGHEST)
    return placed.reshape(tile_count * sketch_tiles.shape[1], sketch_tiles.shape[2]).astype(
        jnp.bfloat16
    )


def widen(placed, split_at):
    out_cols = placed.shape[1]
    upper = jnp.concatenate([placed[:split_at], jnp.zeros((split_at, out_cols), jnp.bfloat16)], 1)
    lower = jnp.concatenate(
        [jnp.zeros((placed.shape[0] - split_at, out_cols), jnp.bfloat16), placed[split_at:]], 1
    )
    return jnp.concatenate([upper, lower], 0)


def per_device(
    acts,
    out_grads,
    lengths,
    in_tiles,
    in_blocks,
    in_signs,
    out_tiles,
    out_blocks,
    out_signs,
    query_grads,
):
    examples_dev, seq_dev, width = acts.shape
    r_in = place(in_tiles, in_blocks, in_signs)
    r_out = widen(place(out_tiles, out_blocks, out_signs), width)
    offset = lax.axis_index("seq") * seq_dev
    positions = offset + jnp.arange(seq_dev, dtype=jnp.int32)
    live_rows = (positions[None, :] < lengths[:, None]).astype(jnp.float32)
    in_sketched = jnp.dot(
        acts.reshape(examples_dev * seq_dev, width), r_in, preferred_element_type=jnp.float32
    )
    in_sketched = (in_sketched.reshape(examples_dev, seq_dev, -1) * live_rows[:, :, None]).astype(
        jnp.bfloat16
    )
    out_sketched = jnp.dot(
        out_grads.reshape(examples_dev * seq_dev, -1), r_out, preferred_element_type=jnp.float32
    )
    out_sketched = out_sketched.reshape(examples_dev, seq_dev, -1).astype(jnp.bfloat16)
    crossed = jnp.einsum(
        "esa,esc->eac", in_sketched, out_sketched, preferred_element_type=jnp.float32
    )
    in_cols = r_in.shape[1] // 2
    out_cols = r_out.shape[1] // 2
    partial_proj = jnp.stack([crossed[:, :in_cols, :out_cols], crossed[:, in_cols:, out_cols:]], 1)
    partial_proj = partial_proj.reshape(examples_dev, -1) / lengths.astype(jnp.float32)[:, None]
    proj_width = partial_proj.shape[1]
    ex_count = lax.axis_size("ex")
    block_width = proj_width // ex_count
    pieces = partial_proj.reshape(examples_dev, ex_count, block_width)
    moved = lax.all_to_all(pieces, "ex", split_axis=1, concat_axis=0, tiled=True)
    summed = lax.psum(moved, "seq")
    owned = summed.astype(jnp.bfloat16).reshape(examples_dev * ex_count, block_width)
    return lax.psum_scatter(
        lax.dot_general(
            owned, query_grads, (((1,), (1,)), ((), ())), preferred_element_type=jnp.float32
        ),
        "ex",
        scatter_dimension=0,
        tiled=True,
    )


def solution(mesh):
    in_specs = (
        P("ex", "seq", None),
        P("ex", "seq", None),
        P("ex"),
        P(),
        P(),
        P(),
        P(),
        P(),
        P(),
        P("seq", "ex"),
    )
    out_specs = P("ex", "seq")
    return jax.shard_map(
        per_device, mesh=mesh, in_specs=in_specs, out_specs=out_specs, check_vma=False
    )
```

profile of v0, /device:TPU:0, one launch (start us, length us, event | category | flops | bytes accessed | tf_op | source)
XLA Modules:
  0.0 92.1 jit_solution(9811729410962465294)
XLA Ops:
  0.0 0.9 add_convert_fusion
  0.9 1.2 %convert_multiply_fusion.1 = f32[40,128,64]{1,2,0:T(8,128)S(1)} fusion(bf16[40,128,64]{1,2,0:T(8,128)(2,1)} %param.16, f32[40,128]{1,0:T(8,128)S(1)} %add_convert_fusion), kind=kLoop, calls=%fused_computation.15 | loop fusion | flops 655360 | bytes 1986560 | tf_op jit(solution)/shard_map/mul | solution.py:12
  2.1 2.3 %convolution_convert_fusion = bf16[40,128,64]{1,0,2:T(8,128)(2,1)S(1)} fusion(f32[40,128,64]{1,2,0:T(8,128)S(1)} %convert_multiply_fusion.1, s32[40]{0:T(128)} %param.17), kind=kOutput, calls=%fused_computation.8 | convolution fusion | flops 157615680 | bytes 1966240 | tf_op jit(solution)/shard_map/bc,bik->cik/dot_general | solution.py:13
  4.5 0.2 copy.39
  4.8 1.0 %fusion.18 = bf16[256,128]{0,1:T(8,128)(2,1)S(1)} fusion(bf16[256,5120]{1,0:T(8,128)(2,1)S(1)} %bitcast.46, bf16[1024,64]{0,1:T(8,128)(2,1)S(1)} %bitcast.54, bf16[4096,64]{0,1:T(8,128)(2,1)S(1)} %bitcast.50), kind=kOutput, calls=%fused_computation.18 | convolution fusion | flops 340819968 | bytes 3342336 | tf_op jit(solution)/shard_map/dot_general | solution.py:52
  5.8 0.1 copy.25
  5.9 1.8 %convert_multiply_fusion = f32[32,128,128]{2,1,0:T(8,128)S(1)} fusion(bf16[32,128,128]{2,1,0:T(8,128)(2,1)} %param.13, f32[32,128]{1,0:T(8,128)S(1)} %add_convert_fusion.1), kind=kLoop, calls=%fused_computation.6 | loop fusion | flops 1048576 | bytes 3162112 | tf_op jit(solution)/shard_map/mul | solution.py:12
  7.8 2.4 %fusion.4 = bf16[32,128,128]{2,0,1:T(8,128)(2,1)S(1)} fusion(f32[32,128,128]{2,1,0:T(8,128)S(1)} %convert_multiply_fusion, s32[32]{0:T(128)S(1)} %copy-done.3), kind=kOutput, calls=%fused_computation.7 | convolution fusion | flops 201851904 | bytes 3145856 | tf_op jit(solution)/shard_map/bc,bik->cik/dot_general | solution.py:13
  10.2 1.4 %copy.21 = bf16[32,128,128]{2,1,0:T(8,128)(2,1)} copy(bf16[32,128,128]{2,0,1:T(8,128)(2,1)S(1)} %fusion.4) | data formatting | bytes 2097152 | tf_op jit(solution)/shard_map/convert_element_type | solution.py:14
  11.6 0.1 compare_convert_fusion
  11.7 2.7 %convolution_bitcast_fusion = f32[16,2,8,128]{3,2,1,0:T(8,128)S(1)} fusion(bf16[4096,128]{1,0:T(8,128)(2,1)} %bitcast.47, bf16[256,4096]{1,0:T(8,128)(2,1)} %bitcast.48), kind=kOutput, calls=%fused_computation.16 | convolution fusion | flops 268435456 | bytes 3276800 | tf_op jit(solution)/shard_map/dot_general | solution.py:46
  14.4 0.1 fusion.23
  14.6 0.1 fusion.38
  14.7 0.1 stack.10
  14.8 0.1 stack.9
  14.9 0.7 maximum_divide_fusion
  15.6 4.3 %all-to-all-start = ((f32[2,2,4096]{2,0,1:T(2,128)}), f32[2,2,4096]{2,0,1:T(2,128)S(1)}, u32[]{:S(2)}, u32[]{:S(2)}) async-start(f32[2,2,4096]{2,0,1:T(2,128)} %maximum_divide_fusion), calls=%async_computation | async-start | bytes 131072 | tf_op jit(solution)/shard_map/all_to_all | solution.py:67
  19.9 0.6 dynamic-slice
  21.1 2.9 %all-to-all-done = f32[2,2,4096]{2,0,1:T(2,128)S(1)} async-done(((f32[2,2,4096]{2,0,1:T(2,128)}), f32[2,2,4096]{2,0,1:T(2,128)S(1)}, u32[]{:S(2)}, u32[]{:S(2)}) %all-to-all-start) | async-done | bytes 65568 | tf_op jit(solution)/shard_map/all_to_all | solution.py:67
  24.0 0.1 all_to_all.16
  24.0 60.9 %psum.7 = bf16[4,1,4096]{2,0,1:T(4,128)(2,1)S(1)} all-reduce(f32[4,1,4096]{2,0,1:T(4,128)S(1)} %all_to_all.16), channel_id=1, replica_groups=mesh['seq'=16,'ex'=2] {'seq'}, use_global_device_ids=true, to_apply=%region_0.0 | all-reduce | flops 16384 | bytes 98304 | tf_op jit(solution)/shard_map/psum | solution.py:68
  85.0 1.6 %fusion.26 = f32[4,128]{1,0:T(4,128)S(1)} fusion(bf16[128,4096]{1,0:T(8,128)(2,1)} %param.19, bf16[4,1,4096]{2,0,1:T(4,128)(2,1)S(1)} %psum.7), kind=kOutput, calls=%fused_computation.27 | convolution fusion | flops 4194304 | bytes 1083392 | tf_op jit(solution)/shard_map/dot_general | solution.py:71
  86.6 4.9 %all-reduce.2 = f32[4,128]{1,0:T(4,128)S(1)} all-reduce(f32[4,128]{1,0:T(4,128)S(1)} %fusion.26), channel_id=2, replica_groups=mesh['seq'=16,'ex'=2] {'ex'}, use_global_device_ids=true, to_apply=%region_1.0.clone | all-reduce | flops 512 | bytes 4096
  91.5 0.6 constant_dynamic-slice_fusion
  (16 shorter events, 0.1 us)
Async XLA Ops:
  0.0 4.7 %copy-start = (bf16[2,128,5120]{2,1,0:T(8,128)(2,1)S(1)}, bf16[2,128,5120]{2,1,0:T(8,128)(2,1)}, u32[]{:S(2)}) copy-start(bf16[2,128,5120]{2,1,0:T(8,128)(2,1)} %param.11) | copy-start | bytes 7864324
  4.7 1.1 %copy-start.1 = (s32[32,128]{1,0:T(8,128)S(1)}, s32[32,128]{1,0:T(8,128)}, u32[]{:S(2)}) copy-start(s32[32,128]{1,0:T(8,128)} %param.15) | copy-start | bytes 49156
  5.8 2.0 %copy-start.3 = (s32[32]{0:T(128)S(1)}, s32[32]{0:T(128)}, u32[]{:S(2)}) copy-start(s32[32]{0:T(128)} %param.14) | copy-start | bytes 388
  7.8 3.9 %copy-start.2 = (s32[2]{0:T(128)S(1)}, s32[2]{0:T(128)}, u32[]{:S(2)}) copy-start(s32[2]{0:T(128)} %param.12) | copy-start | bytes 28
  11.7 8.2 %copy-start.4 = (u32[32]{0:T(128)S(1)}, u32[32]{0:T(128)}, u32[]{:S(2)}) copy-start(u32[32]{0:T(128)} %constant.25) | copy-start | bytes 388
  15.6 8.4 %all-to-all-start = ((f32[2,2,4096]{2,0,1:T(2,128)}), f32[2,2,4096]{2,0,1:T(2,128)S(1)}, u32[]{:S(2)}, u32[]{:S(2)}) async-start(f32[2,2,4096]{2,0,1:T(2,128)} %maximum_divide_fusion), calls=%async_computation | async-start | bytes 131072 | tf_op jit(solution)/shard_map/all_to_all | solution.py:67
where the time goes:
time: 92.4 us; the launch traced here: 92.1 us
  blocking collectives  65.9 us (71%)
  matrix products  10.2 us (11%)
  other arithmetic  4.75 us (5%)
  starting transfers between devices  4.26 us (5%)
  local copies, waits for them, and re-layouts  3.29 us (4%)
  waiting for transfers between devices  2.89 us (3%)
    psum x1, blocking collectives, per_device(): summed = lax.psum(moved, 'seq')  60.9 us
    unnamed x1, blocking collectives  4.93 us
    dot_general x2, matrix products, place(): jnp.einsum('bc,bik->cik', chosen, signed, precision=lax.Precision.HIGHEST)  4.72 us
    all_to_all x1, starting transfers between devices, per_device(): lax.all_to_all(pieces, 'ex', split_axis=1, concat_axis=0, tiled=True)  4.26 us
    mul x2, other arithmetic, place(): sketch_tiles.astype(jnp.float32)  3.08 us
    all_to_all x1, waiting for transfers between devices, per_device(): lax.all_to_all(pieces, 'ex', split_axis=1, concat_axis=0, tiled=True)  2.89 us
    dot_general x1, matrix products, per_device(): jnp.dot(acts.reshape(examples_dev * seq_dev, width), r_in, preferred_elem...  2.74 us
  transfers between devices with their start and end apart: 1, of which 1 were waited for; matrix products, arithmetic and copies ran while one was open for 1% of the time, Pallas kernels for 0%

commit v1 on v0

--- a/solution.py
+++ b/solution.py
@@ -2,6 +2,15 @@
 import jax.numpy as jnp
 from jax import lax
 from jax.sharding import PartitionSpec as P
+
+
+def added_up(shard, name):
+    size = lax.axis_size(name)
+    result, far = (shard, 1)
+    while far < size:
+        result = result + lax.ppermute(result, name, [(i, i ^ far) for i in range(size)])
+        far = 2 * far
+    return result
 
 
 def place(sketch_tiles, block_ids, sign_bits):
@@ -65,7 +74,7 @@
     block_width = proj_width // ex_count
     pieces = partial_proj.reshape(examples_dev, ex_count, block_width)
     moved = lax.all_to_all(pieces, "ex", split_axis=1, concat_axis=0, tiled=True)
-    summed = lax.psum(moved, "seq")
+    summed = added_up(moved, "seq")
     owned = summed.astype(jnp.bfloat16).reshape(examples_dev * ex_count, block_width)
     return lax.psum_scatter(
         lax.dot_general(

time: 92.4 us -> 45.9 us (0.50)
  blocking collectives: 65.9 us -> 13.1 us
  waiting for transfers between devices: 2.89 us -> 8.04 us
  starting transfers between devices: 4.26 us -> 5.92 us
    psum x1 -> x0, blocking collectives: 60.9 us -> none  [per_device(): summed = lax.psum(moved, 'seq')]
    all_to_all x0 -> x1, blocking collectives: none -> 8.19 us  [per_device(): lax.all_to_all(pieces, 'ex', split_axis=1, concat_axis=0, tiled=True)]
    ppermute x0 -> x4, waiting for transfers between devices: none -> 8.04 us  [added_up(): lax.ppermute(result, name, [(i, i ^ far) for i in range(size)])]
    ppermute x0 -> x4, starting transfers between devices: none -> 5.92 us  [added_up(): lax.ppermute(result, name, [(i, i ^ far) for i in range(size)])]
    all_to_all x1 -> x0, starting transfers between devices: 4.26 us -> none  [per_device(): lax.all_to_all(pieces, 'ex', split_axis=1, concat_axis=0, tiled=True)]
    all_to_all x1 -> x0, waiting for transfers between devices: 2.89 us -> none  [per_device(): lax.all_to_all(pieces, 'ex', split_axis=1, concat_axis=0, tiled=True)]
  transfers between devices with their start and end apart: 1 -> 4, of which waited for: 1 -> 4; matrix products, arithmetic and copies ran while one was open for 1% -> 1% of each run, Pallas kernels for 0% -> 0%
where the time goes in v1:
time: 45.9 us; the launch traced here: 45.6 us
  blocking collectives  13.1 us (29%)
  matrix products  10.2 us (22%)
  waiting for transfers between devices  8.04 us (18%)
  starting transfers between devices  5.92 us (13%)
  other arithmetic  4.19 us (9%)
  local copies, waits for them, and re-layouts  3.28 us (7%)
  between operations  0.85 us (2%)
    all_to_all x1, blocking collectives, per_device(): lax.all_to_all(pieces, 'ex', split_axis=1, concat_axis=0, tiled=True)  8.19 us
    ppermute x4, waiting for transfers between devices, added_up(): lax.ppermute(result, name, [(i, i ^ far) for i in range(size)])  8.04 us
    ppermute x4, starting transfers between devices, added_up(): lax.ppermute(result, name, [(i, i ^ far) for i in range(size)])  5.92 us
    unnamed x1, blocking collectives  4.93 us
    dot_general x2, matrix products, place(): jnp.einsum('bc,bik->cik', chosen, signed, precision=lax.Precision.HIGHEST)  4.72 us
    mul x2, other arithmetic, place(): sketch_tiles.astype(jnp.float32)  3.08 us
    dot_general x1, matrix products, per_device(): jnp.dot(acts.reshape(examples_dev * seq_dev, width), r_in, preferred_elem...  2.74 us
    dot_general x1, matrix products, per_device(): lax.dot_general(owned, query_grads, (((1,), (1,)), ((), ())), preferred_e...  1.59 us
  transfers between devices with their start and end apart: 4, of which 4 were waited for; matrix products, arithmetic and copies ran while one was open for 1% of the time, Pallas kernels for 0%

profile of v1, /device:TPU:0, one launch (start us, length us, event | category | flops | bytes accessed | tf_op | source)
XLA Modules:
  0.0 45.6 jit_solution(4581415204456315485)
XLA Ops:
  0.0 0.9 %add_convert_fusion.1 = f32[40,128]{1,0:T(8,128)S(1)} fusion(s32[40,128]{1,0:T(8,128)} %param.18), kind=kLoop, calls=%fused_computation.30 | loop fusion | flops 15360 | bytes 40960 | tf_op jit(solution)/shard_map/convert_element_type | solution.py:21
  0.9 1.2 %convert_multiply_fusion.1 = f32[40,128,64]{1,2,0:T(8,128)S(1)} fusion(bf16[40,128,64]{1,2,0:T(8,128)(2,1)} %param.16, f32[40,128]{1,0:T(8,128)S(1)} %add_convert_fusion.1), kind=kLoop, calls=%fused_computation.15 | loop fusion | flops 655360 | bytes 1986560 | tf_op jit(solution)/shard_map/mul | solution.py:21
  2.1 2.3 %convolution_convert_fusion = bf16[40,128,64]{1,0,2:T(8,128)(2,1)S(1)} fusion(f32[40,128,64]{1,2,0:T(8,128)S(1)} %convert_multiply_fusion.1, s32[40]{0:T(128)} %param.17), kind=kOutput, calls=%fused_computation.8 | convolution fusion | flops 157615680 | bytes 1966240 | tf_op jit(solution)/shard_map/bc,bik->cik/dot_general | solution.py:22
  4.5 0.2 copy.39
  4.8 1.0 %fusion.18 = bf16[256,128]{0,1:T(8,128)(2,1)S(1)} fusion(bf16[256,5120]{1,0:T(8,128)(2,1)S(1)} %bitcast.46, bf16[1024,64]{0,1:T(8,128)(2,1)S(1)} %bitcast.54, bf16[4096,64]{0,1:T(8,128)(2,1)S(1)} %bitcast.50), kind=kOutput, calls=%fused_computation.18 | convolution fusion | flops 340819968 | bytes 3342336 | tf_op jit(solution)/shard_map/dot_general | solution.py:61
  5.8 0.1 copy.25
  5.9 1.8 %convert_multiply_fusion = f32[32,128,128]{2,1,0:T(8,128)S(1)} fusion(bf16[32,128,128]{2,1,0:T(8,128)(2,1)} %param.13, f32[32,128]{1,0:T(8,128)S(1)} %add_convert_fusion.2), kind=kLoop, calls=%fused_computation.6 | loop fusion | flops 1048576 | bytes 3162112 | tf_op jit(solution)/shard_map/mul | solution.py:21
  7.8 2.4 %fusion.4 = bf16[32,128,128]{2,0,1:T(8,128)(2,1)S(1)} fusion(f32[32,128,128]{2,1,0:T(8,128)S(1)} %convert_multiply_fusion, s32[32]{0:T(128)S(1)} %copy-done.3), kind=kOutput, calls=%fused_computation.7 | convolution fusion | flops 201851904 | bytes 3145856 | tf_op jit(solution)/shard_map/bc,bik->cik/dot_general | solution.py:22
  10.2 1.4 %copy.21 = bf16[32,128,128]{2,1,0:T(8,128)(2,1)} copy(bf16[32,128,128]{2,0,1:T(8,128)(2,1)S(1)} %fusion.4) | data formatting | bytes 2097152 | tf_op jit(solution)/shard_map/convert_element_type | solution.py:23
  11.7 2.7 %convolution_bitcast_fusion = f32[16,2,8,128]{3,2,1,0:T(8,128)S(1)} fusion(bf16[4096,128]{1,0:T(8,128)(2,1)} %bitcast.47, bf16[256,4096]{1,0:T(8,128)(2,1)} %bitcast.48), kind=kOutput, calls=%fused_computation.16 | convolution fusion | flops 268435456 | bytes 3276800 | tf_op jit(solution)/shard_map/dot_general | solution.py:55
  14.4 0.1 fusion.23
  14.7 0.1 stack.10
  15.0 8.2 %all_to_all.18 = f32[2,2,4096]{2,0,1:T(2,128)S(1)} all-to-all(f32[2,2,4096]{2,0,1:T(2,128)S(1)} %maximum_divide_fusion), channel_id=1, replica_groups=mesh['seq'=16,'ex'=2] {'ex'}, dimensions={1} | all-to-all | bytes 131072 | tf_op jit(solution)/shard_map/all_to_all | solution.py:76
  23.3 1.2 %collective-permute-done = f32[4,1,4096]{2,0,1:T(4,128)S(1)} collective-permute-done((f32[4,1,4096]{2,0,1:T(4,128)S(1)}, f32[4,1,4096]{2,0,1:T(4,128)S(1)}, u32[]{:S(2)}, u32[]{:S(2)}) %collective-permute-start) | collective-permute-done | bytes 65568 | tf_op jit(solution)/shard_map/ppermute | solution.py:11
  24.6 1.6 %collective-permute-start.1 = (f32[4,1,4096]{2,0,1:T(4,128)S(1)}, f32[4,1,4096]{2,0,1:T(4,128)S(1)}, u32[]{:S(2)}, u32[]{:S(2)}) collective-permute-start(f32[4,1,4096]{2,0,1:T(4,128)S(1)} %add.32), channel_id=1, source_target_pairs={{0,4},{2,6},{4,0},{6,2},{8,12},{10,14},{12,8},{14,10},{16,20},{18,... | collective-permute-start | bytes 196616 | tf_op jit(solution)/shard_map/ppermute | solution.py:11
  26.1 2.8 %collective-permute-done.1 = f32[4,1,4096]{2,0,1:T(4,128)S(1)} collective-permute-done((f32[4,1,4096]{2,0,1:T(4,128)S(1)}, f32[4,1,4096]{2,0,1:T(4,128)S(1)}, u32[]{:S(2)}, u32[]{:S(2)}) %collective-permute-start.1) | collective-permute-done | bytes 65568 | tf_op jit(solution)/shard_map/ppermute | solution.py:11
  28.9 1.6 %collective-permute-start.2 = (f32[4,1,4096]{2,0,1:T(4,128)S(1)}, f32[4,1,4096]{2,0,1:T(4,128)S(1)}, u32[]{:S(2)}, u32[]{:S(2)}) collective-permute-start(f32[4,1,4096]{2,0,1:T(4,128)S(1)} %add.33), channel_id=1, source_target_pairs={{0,8},{2,10},{4,12},{6,14},{8,0},{10,2},{12,4},{14,6},{16,24},{18,... | collective-permute-start | bytes 196616 | tf_op jit(solution)/shard_map/ppermute | solution.py:11
  30.6 2.7 %collective-permute-done.2 = f32[4,1,4096]{2,0,1:T(4,128)S(1)} collective-permute-done((f32[4,1,4096]{2,0,1:T(4,128)S(1)}, f32[4,1,4096]{2,0,1:T(4,128)S(1)}, u32[]{:S(2)}, u32[]{:S(2)}) %collective-permute-start.2) | collective-permute-done | bytes 65568 | tf_op jit(solution)/shard_map/ppermute | solution.py:11
  33.3 2.7 %collective-permute-start.3 = (f32[4,1,4096]{2,0,1:T(4,128)S(1)}, f32[4,1,4096]{2,0,1:T(4,128)S(1)}, u32[]{:S(2)}, u32[]{:S(2)}) collective-permute-start(f32[4,1,4096]{2,0,1:T(4,128)S(1)} %add.34), channel_id=1, source_target_pairs={{0,16},{2,18},{4,20},{6,22},{8,24},{10,26},{12,28},{14,30},{16,0},... | collective-permute-start | bytes 196616 | tf_op jit(solution)/shard_map/ppermute | solution.py:11
  35.9 0.6 %dynamic-slice = u32[1]{0:T(128)} dynamic-slice(u32[32]{0:T(128)S(1)} %copy-done.4, u32[]{:T(128)S(6)} %add.37), dynamic_slice_sizes={1} | dynamic-slice | bytes 12
  37.2 1.3 %collective-permute-done.3 = f32[4,1,4096]{2,0,1:T(4,128)S(1)} collective-permute-done((f32[4,1,4096]{2,0,1:T(4,128)S(1)}, f32[4,1,4096]{2,0,1:T(4,128)S(1)}, u32[]{:S(2)}, u32[]{:S(2)}) %collective-permute-start.3) | collective-permute-done | bytes 65568 | tf_op jit(solution)/shard_map/ppermute | solution.py:11
  38.5 1.6 %fusion.27 = f32[4,128]{1,0:T(4,128)S(1)} fusion(bf16[128,4096]{1,0:T(8,128)(2,1)} %param.19, f32[4,1,4096]{2,0,1:T(4,128)S(1)} %add.34, f32[4,1,4096]{2,0,1:T(4,128)S(1)} %collective-permute-done.3), kind=kOutput, calls=%fused_computation.29 | convolution fusion | flops 4227072 | bytes 1181696 | tf_op jit(solution)/shard_map/dot_general | solution.py:80
  40.1 4.9 %all-reduce.2 = f32[4,128]{1,0:T(4,128)S(1)} all-reduce(f32[4,128]{1,0:T(4,128)S(1)} %fusion.27), channel_id=2, replica_groups=mesh['seq'=16,'ex'=2] {'ex'}, use_global_device_ids=true, to_apply=%region_0.0.clone | all-reduce | flops 512 | bytes 4096
  45.0 0.6 %constant_dynamic-slice_fusion = f32[2,128]{1,0:T(2,128)} fusion(f32[4,128]{1,0:T(4,128)S(1)} %all-reduce.2, u32[]{:T(128)S(6)} %multiply.1), kind=kLoop, calls=%fused_computation.39 | loop fusion | bytes 2052
  (25 shorter events, 0.6 us)
Async XLA Ops:
  0.0 4.7 %copy-start = (bf16[2,128,5120]{2,1,0:T(8,128)(2,1)S(1)}, bf16[2,128,5120]{2,1,0:T(8,128)(2,1)}, u32[]{:S(2)}) copy-start(bf16[2,128,5120]{2,1,0:T(8,128)(2,1)} %param.11) | copy-start | bytes 7864324
  4.7 1.1 %copy-start.1 = (s32[32,128]{1,0:T(8,128)S(1)}, s32[32,128]{1,0:T(8,128)}, u32[]{:S(2)}) copy-start(s32[32,128]{1,0:T(8,128)} %param.15) | copy-start | bytes 49156
  5.8 2.0 %copy-start.3 = (s32[32]{0:T(128)S(1)}, s32[32]{0:T(128)}, u32[]{:S(2)}) copy-start(s32[32]{0:T(128)} %param.14) | copy-start | bytes 388
  7.8 3.8 %copy-start.2 = (s32[2]{0:T(128)S(1)}, s32[2]{0:T(128)}, u32[]{:S(2)}) copy-start(s32[2]{0:T(128)} %param.12) | copy-start | bytes 28
  11.7 24.2 %copy-start.4 = (u32[32]{0:T(128)S(1)}, u32[32]{0:T(128)}, u32[]{:S(2)}) copy-start(u32[32]{0:T(128)} %constant.25) | copy-start | bytes 388
  23.2 1.3 %collective-permute-start = (f32[4,1,4096]{2,0,1:T(4,128)S(1)}, f32[4,1,4096]{2,0,1:T(4,128)S(1)}, u32[]{:S(2)}, u32[]{:S(2)}) collective-permute-start(f32[4,1,4096]{2,0,1:T(4,128)S(1)} %all_to_all.16), channel_id=1, source_target_pairs={{0,2},{2,0},{4,6},{6,4},{8,10},{10,8},{12,14},{14,12},{16,18},{18,... | collective-permute-start | bytes 196616 | tf_op jit(solution)/shard_map/ppermute | solution.py:11
  24.6 4.3 %collective-permute-start.1 = (f32[4,1,4096]{2,0,1:T(4,128)S(1)}, f32[4,1,4096]{2,0,1:T(4,128)S(1)}, u32[]{:S(2)}, u32[]{:S(2)}) collective-permute-start(f32[4,1,4096]{2,0,1:T(4,128)S(1)} %add.32), channel_id=1, source_target_pairs={{0,4},{2,6},{4,0},{6,2},{8,12},{10,14},{12,8},{14,10},{16,20},{18,... | collective-permute-start | bytes 196616 | tf_op jit(solution)/shard_map/ppermute | solution.py:11
  28.9 4.3 %collective-permute-start.2 = (f32[4,1,4096]{2,0,1:T(4,128)S(1)}, f32[4,1,4096]{2,0,1:T(4,128)S(1)}, u32[]{:S(2)}, u32[]{:S(2)}) collective-permute-start(f32[4,1,4096]{2,0,1:T(4,128)S(1)} %add.33), channel_id=1, source_target_pairs={{0,8},{2,10},{4,12},{6,14},{8,0},{10,2},{12,4},{14,6},{16,24},{18,... | collective-permute-start | bytes 196616 | tf_op jit(solution)/shard_map/ppermute | solution.py:11
  33.3 5.2 %collective-permute-start.3 = (f32[4,1,4096]{2,0,1:T(4,128)S(1)}, f32[4,1,4096]{2,0,1:T(4,128)S(1)}, u32[]{:S(2)}, u32[]{:S(2)}) collective-permute-start(f32[4,1,4096]{2,0,1:T(4,128)S(1)} %add.34), channel_id=1, source_target_pairs={{0,16},{2,18},{4,20},{6,22},{8,24},{10,26},{12,28},{14,30},{16,0},... | collective-permute-start | bytes 196616 | tf_op jit(solution)/shard_map/ppermute | solution.py:11
